TPU v7x, 256 devices: a whole 4x4x8 slice. The times are simulated.
256 devices in a mesh: dp: 2 (over z_lo), seq: 32 (over y, x, core), head: 4 (over z_hi).
Axes of the slice: x: 4, y: 4, z: 8 (z_hi: 4, z_lo: 2; z = z_hi * 2 + z_lo), core: 2. Of those that a mesh axis runs over, the one named last changes fastest.
Arguments:
- query_rows: bfloat16 [2, 8192, 4096], P('dp', 'seq', 'head'), may hold values from -0.59765625 to 0.59765625
- key_rows: bfloat16 [2, 8192, 4096], P('dp', 'seq', 'head'), may hold values from -0.59765625 to 0.59765625
- value_rows: bfloat16 [2, 8192, 4096], P('dp', 'seq', 'head'), may hold values from -1536 to 1536
- grad_out: bfloat16 [2, 8192, 6144], P('dp', 'seq'), may hold values from -6 to 6
- out_weight: bfloat16 [6144, 4096], P('seq', 'head'), may hold values from -0.09375 to 0.09375
- decay_rates: float32 [32], P('head'), may hold values from 0 to 1, as said below
- doc_blocks: int32 [2, 64], P('dp'), may hold values from 0 to 7, never falling along the last dimension, each value on 1 to 32 neighbouring positions
Outputs:
- grad_query: bfloat16 [2, 8192, 4096], P('dp', 'seq', 'head')
- grad_key: bfloat16 [2, 8192, 4096], P('dp', 'seq', 'head')
- grad_value: bfloat16 [2, 8192, 4096], P('dp', 'seq', 'head')
- grad_weight: float32 [6144, 4096], P('seq', 'head')
Inputs may be any that keep to these rules, and one draw needn't show every extreme that they name: `doc_blocks`: in each pack document numbers never fall from block to block; every document covers 1 to 32 blocks, and one covers exactly 32. `decay_rates`: rates are positive.
All inputs are finite; a program needn't handle non-finite values.
Results may differ from a plain program's by a relative error of at most 0.024.
Values may be sent and summed in bfloat16 or wider, within the bound.
No kernel may reach another device: no remote copies, remote signals or barrier semaphores. Data moves between devices by JAX's collectives and lax.ppermute only.
A program may use at most 192 MiB of HBM per device.

v0:
```python
import jax
import jax.numpy as jnp
from jax import lax
from jax.sharding import PartitionSpec as P

BLOCK = 128
EPSILON = 1e-05


def prefix(array, axis, join, neutral, backward):
    count = lax.axis_size(axis)
    place = lax.axis_index(axis)
    ahead = count - 1 - place if backward else place
    gathered = jax.tree.map(
        lambda a, kind: lax.all_gather(a.astype(kind), axis), array, (jnp.bfloat16, jnp.bfloat16)
    )
    state = jax.tree.map(lambda a, e: jnp.zeros_like(a) + jnp.asarray(e, a.dtype), array, neutral)

    def one(step, state):
        source = count - 1 - step if backward else step
        return join(
            state,
            jax.tree.map(
                lambda a, own: lax.dynamic_index_in_dim(a, source, 0, False).astype(own.dtype),
                gathered,
                array,
            ),
        )

    return lax.fori_loop(0, ahead, one, state)


def block_docs(doc_row, first_block, block_count, block_len):
    blocks = lax.dynamic_slice_in_dim(doc_row, first_block, block_count)
    return jnp.reshape(
        jnp.broadcast_to(blocks[:, None], (block_count, block_len)), (block_count * block_len,)
    )


def decay_masks(token_docs, decay_rates, prev_doc, next_doc):
    length = token_docs.shape[0]
    position = jnp.arange(length).astype(jnp.float32)
    rates = decay_rates[:, None]
    distance = position[:, None] - position[None, :]
    allowed = jnp.logical_and(distance >= 0, token_docs[:, None] == token_docs[None, :])
    intra = jnp.where(
        allowed[None], jnp.exp(-rates[:, :, None] * jnp.maximum(distance, 0.0)[None]), 0.0
    )
    weight_end = jnp.where(
        (token_docs == token_docs[length - 1])[None],
        jnp.exp(-rates * (length - 1.0 - position)[None]),
        0.0,
    )
    weight_start = jnp.where(
        (token_docs == token_docs[0])[None], jnp.exp(-rates * position[None]), 0.0
    )
    weight_before = jnp.where(
        (token_docs == prev_doc)[None], jnp.exp(-rates * (position + 1.0)[None]), 0.0
    )
    weight_after = jnp.where(
        (token_docs == next_doc)[None], jnp.exp(-rates * (length - position)[None]), 0.0
    )
    span_decay = jnp.exp(-decay_rates * float(length))
    link_fwd = jnp.where(token_docs[length - 1] == prev_doc, span_decay, 0.0)
    link_rev = jnp.where(token_docs[0] == next_doc, span_decay, 0.0)
    return (intra, weight_end, weight_start, weight_before, weight_after, link_fwd, link_rev)


def combine_states(earlier, later):
    return (earlier[0] * later[0], later[0][:, None, None] * earlier[1] + later[1])


def local_state(keys_here, values_here, weight_end):
    weighted = (keys_here.astype(jnp.float32) * weight_end.T[:, :, None]).astype(jnp.bfloat16)
    return jnp.einsum("jhd,jhe->hde", weighted, values_here, preferred_element_type=jnp.float32)


def forward_out(queries, keys_here, values_here, intra, weight_before, state_in):
    scores = jnp.einsum("thd,jhd->htj", queries, keys_here, preferred_element_type=jnp.float32)
    attention = (scores * intra).astype(jnp.bfloat16)
    state_low = state_in.astype(jnp.bfloat16)
    carried = jnp.einsum("thd,hde->the", queries, state_low, preferred_element_type=jnp.float32)
    output = (
        jnp.einsum("htj,jhe->the", attention, values_here, preferred_element_type=jnp.float32)
        + weight_before.T[:, :, None] * carried
    )
    inverse_rms = lax.rsqrt(jnp.mean(output * output, axis=-1, keepdims=True) + EPSILON)
    return (attention, state_low, output * inverse_rms, inverse_rms)


def backward_local(queries, values_here, intra, normal, inverse_rms, grad_normed, weight_start):
    inner = jnp.mean(grad_normed * normal, axis=-1, keepdims=True)
    grad_attn = (inverse_rms * (grad_normed - normal * inner)).astype(jnp.bfloat16)
    grad_scores = (
        jnp.einsum("the,jhe->htj", grad_attn, values_here, preferred_element_type=jnp.float32)
        * intra
    ).astype(jnp.bfloat16)
    weighted = (queries.astype(jnp.float32) * weight_start.T[:, :, None]).astype(jnp.bfloat16)
    back_local = jnp.einsum("thd,the->hde", weighted, grad_attn, preferred_element_type=jnp.float32)
    return (grad_attn, grad_scores, back_local)


def backward_rest(
    queries,
    keys_here,
    values_here,
    attention,
    state_low,
    grad_attn,
    grad_scores,
    weight_before,
    weight_after,
    state_back,
):
    back_low = state_back.astype(jnp.bfloat16)
    grad_query = jnp.einsum(
        "htj,jhd->thd", grad_scores, keys_here, preferred_element_type=jnp.float32
    ) + weight_before.T[:, :, None] * jnp.einsum(
        "the,hde->thd", grad_attn, state_low, preferred_element_type=jnp.float32
    )
    grad_key = jnp.einsum(
        "htj,thd->jhd", grad_scores, queries, preferred_element_type=jnp.float32
    ) + weight_after.T[:, :, None] * jnp.einsum(
        "jhe,hde->jhd", values_here, back_low, preferred_element_type=jnp.float32
    )
    grad_value = jnp.einsum(
        "htj,the->jhe", attention, grad_attn, preferred_element_type=jnp.float32
    ) + weight_after.T[:, :, None] * jnp.einsum(
        "jhd,hde->jhe", keys_here, back_low, preferred_element_type=jnp.float32
    )
    return (
        grad_query.astype(jnp.bfloat16),
        grad_key.astype(jnp.bfloat16),
        grad_value.astype(jnp.bfloat16),
    )


def local(query_rows, key_rows, value_rows, grad_out, out_weight, decay_rates, doc_blocks):
    tok_count = query_rows.shape[1]
    heads_here = decay_rates.shape[0]
    head_dim = query_rows.shape[2] // heads_here
    seq_count = lax.axis_size("seq")
    span_index = lax.axis_index("seq")
    block_count = tok_count // BLOCK
    total_blocks = doc_blocks.shape[1]
    queries = query_rows[0].reshape(tok_count, heads_here, head_dim)
    keys_here = key_rows[0].reshape(tok_count, heads_here, head_dim)
    values_here = value_rows[0].reshape(tok_count, heads_here, head_dim)
    grad_rows = grad_out[0]
    doc_row = doc_blocks[0]
    first_block = span_index * block_count
    token_docs = block_docs(doc_row, first_block, block_count, BLOCK)
    prev_doc = doc_row[jnp.maximum(first_block - 1, 0)]
    next_doc = doc_row[jnp.minimum(first_block + block_count, total_blocks - 1)]
    intra, weight_end, weight_start, weight_before, weight_after, link_fwd, link_rev = decay_masks(
        token_docs, decay_rates, prev_doc, next_doc
    )
    state_local = local_state(keys_here, values_here, weight_end)
    identity = (jnp.ones_like(link_fwd), jnp.zeros_like(state_local))
    state_in = prefix((link_fwd, state_local), "seq", combine_states, identity, False)[1]
    attention, state_low, normal, inverse_rms = forward_out(
        queries, keys_here, values_here, intra, weight_before, state_in
    )
    columns = grad_rows
    grad_normed = jnp.dot(
        columns,
        lax.all_gather(out_weight, "seq", axis=0, tiled=True),
        preferred_element_type=jnp.float32,
    )
    normed = normal.astype(jnp.bfloat16).reshape(tok_count, heads_here * head_dim)
    columns = grad_rows
    part = lax.dot_general(
        columns, normed, (((0,), (0,)), ((), ())), preferred_element_type=jnp.float32
    )
    weight_part = lax.psum_scatter(
        part.astype(jnp.bfloat16).astype(jnp.float32).astype(jnp.bfloat16),
        "seq",
        scatter_dimension=0,
        tiled=True,
    )
    norm_factor = (lax.axis_size("dp") * seq_count * tok_count) ** (-0.5)
    grad_weight = lax.psum(weight_part, "dp").astype(jnp.float32) * norm_factor
    grad_attn, grad_scores, back_local = backward_local(
        queries,
        values_here,
        intra,
        normal,
        inverse_rms,
        grad_normed.reshape(tok_count, heads_here, head_dim),
        weight_start,
    )
    back_identity = (jnp.ones_like(link_rev), jnp.zeros_like(back_local))
    state_back = prefix((link_rev, back_local), "seq", combine_states, back_identity, True)[1]
    grad_query, grad_key, grad_value = backward_rest(
        queries,
        keys_here,
        values_here,
        attention,
        state_low,
        grad_attn,
        grad_scores,
        weight_before,
        weight_after,
        state_back,
    )
    flat_shape = (1, tok_count, heads_here * head_dim)
    return (
        grad_query.reshape(flat_shape),
        grad_key.reshape(flat_shape),
        grad_value.reshape(flat_shape),
        grad_weight,
    )


def solution(mesh):
    in_specs = (
        P("dp", "seq", "head"),
        P("dp", "seq", "head"),
        P("dp", "seq", "head"),
        P("dp", "seq", None),
        P("seq", "head"),
        P("head"),
        P("dp", None),
    )
    out_specs = (
        P("dp", "seq", "head"),
        P("dp", "seq", "head"),
        P("dp", "seq", "head"),
        P("seq", "head"),
    )
    return jax.shard_map(local, mesh=mesh, in_specs=in_specs, out_specs=out_specs, check_vma=False)
```

profile of v0, /device:TPU:1, one launch (start us, length us, event | category | flops | bytes accessed | tf_op | source)
XLA Modules:
  0.0 419.0 jit_solution(4983138501228653416)
XLA Ops:
  12.7 2.7 bitcast_compare_fusion.3
  15.4 1.9 copy.85
  17.3 2.1 copy.58
  21.4 2.0 convolution_convert_fusion.1
  26.0 66.1 %all-reduce.2 = (bf16[256]{0:T(256)(128)(2,1)S(1)}, bf16[256]{0:T(256)(128)(2,1)S(1)}) all-reduce(bf16[256]{0:T(256)(128)(2,1)S(1)} %dynamic-update-slice, bf16[256]{0:T(256)(128)(2,1)S(1)} %dynamic-update-slice.1), channel_id=2, replica_groups=mesh['dp'=2,'seq'=32,'head'=4] {'seq'}, use_global_device_ids=true, to_apply=%add | all-reduce | flops 512 | bytes 2048
  92.1 2.1 copy.84
  99.7 2.1 while.26
  99.7 2.1 convert_add_fusion.4
  101.8 3.0 multiply_reduce_fusion.1
  104.7 51.4 %all-gather.8.cloned.1.call-done = bf16[6144,1024]{1,0:T(8,128)(2,1)} async-done(((bf16[192,1024]{1,0:T(8,128)(2,1)}), bf16[6144,1024]{1,0:T(8,128)(2,1)}) %all-gather.8.cloned.1.call-update) | async-done | bytes 12582928 | tf_op jit(solution)/shard_map/all_gather | solution.py:167
  156.1 16.7 %copy.62 = bf16[1024,6144]{1,0:T(8,128)(2,1)} copy(bf16[1024,6144]{0,1:T(8,128)(2,1)} %bitcast.111) | data formatting | bytes 25165824 | tf_op jit(solution)/shard_map/dot_general | solution.py:165
  172.8 7.0 %multiply_reduce_fusion = (f32[256,8]{0,1:T(8,128)S(1)}, f32[256,8,128]{0,2,1:T(8,128)S(1)}) fusion(f32[256,8,128]{0,2,1:T(8,128)} %get-tuple-element.186, f32[256,8]{0,1:T(8,128)S(1)} %add_rsqrt_fusion, bf16[8,128,6144]{2,1,0:T(8,128)(2,1)} %bitcast.112, bf16[1,256,6144]{2,1,0:T(8,128)(2,1)S(1)} %copy-done), kind=kOutput, calls=%fused_computation.35 | convolution fusion | flops 3222009856 | bytes 17842176 | tf_op jit(solution)/shard_map/dot_general | solution.py:165
  182.8 7.4 %convert_bitcast_fusion = bf16[6144,1024]{0,1:T(8,128)(2,1)} fusion(bf16[256,1024]{0,1:T(8,128)(2,1)} %bitcast.127, bf16[1,256,6144]{2,1,0:T(8,128)(2,1)S(1)} %copy-done), kind=kOutput, calls=%fused_computation.4 | convolution fusion | flops 3227516928 | bytes 16252928 | tf_op jit(solution)/shard_map/dot_general | solution.py:172
  190.2 16.7 %copy.82 = bf16[6144,1024]{1,0:T(8,128)(2,1)} copy(bf16[6144,1024]{0,1:T(8,128)(2,1)} %convert_bitcast_fusion) | data formatting | bytes 25165824
  213.4 37.4 %all-gather.12.cloned.1.call-done = bf16[256,128,128]{2,1,0:T(8,128)(2,1)} async-done(((bf16[8,128,128]{2,1,0:T(8,128)(2,1)}), bf16[256,128,128]{2,1,0:T(8,128)(2,1)}) %all-gather.12.cloned.1.call-update) | async-done | bytes 8388624 | tf_op jit(solution)/shard_map/all_gather | solution.py:15
  250.9 35.0 %while.27 = (s32[]{:T(128)}, f32[8,128,128]{2,1,0:T(8,128)S(1)}, s32[]{:T(128)}, bf16[32,8]{1,0:T(8,128)(2,1)S(1)}, bf16[32,8,128,128]{3,2,1,0:T(8,128)(2,1)}, /*index=5*/s32[]{:T(128)}, s32[]{:T(128)}, s32[]{:T(128)}, s32[]{:T(128)}) while((s32[]{:T(128)}, f32[8,128,128]{2,1,0:T(8,128)S(1)}, s32[]{:T(128)}, bf16[32,8]{1,0:T(8,128)(2,1)S(1)}, ...), condition=%wide.region_5.6_spmd, body=%wide.region_4.5_spmd.sunk | while | flops 393230 | bytes 1310955 | solution.py:30
  285.9 79.1 %reduce-scatter.4.cloned.1.call-done = bf16[192,1024]{1,0:T(8,128)(2,1)} async-done(((bf16[6144,1024]{1,0:T(8,128)(2,1)}), bf16[192,1024]{1,0:T(8,128)(2,1)}) %reduce-scatter.4.cloned.1.call-update) | async-done | bytes 393232
  364.9 2.0 copy.83
  368.1 2.2 copy.75
  370.3 2.7 fusion.12
  373.0 2.0 copy.74
  375.0 32.9 %all-reduce.5.cloned.1.call-done = bf16[192,1024]{0,1:T(8,128)(2,1)} async-done(((bf16[192,1024]{0,1:T(8,128)(2,1)}), bf16[192,1024]{0,1:T(8,128)(2,1)}) %all-reduce.5.cloned.1.call-update) | async-done | bytes 393232 | tf_op jit(solution)/shard_map/psum | solution.py:182
  408.0 2.1 convert_multiply_fusion
  410.0 2.4 copy.76
  (148 shorter events, 56.9 us)
Async XLA Ops:
  7.2 165.6 %copy-start = (bf16[1,256,6144]{2,1,0:T(8,128)(2,1)S(1)}, bf16[1,256,6144]{2,1,0:T(8,128)(2,1)}, u32[]{:S(2)}) copy-start(bf16[1,256,6144]{2,1,0:T(8,128)(2,1)} %param.14) | copy-start | bytes 9437188
  7.2 17.1 %copy-start.20 = (u32[256]{0:T(256)S(1)}, u32[256]{0:T(256)}, u32[]{:S(2)}) copy-start(u32[256]{0:T(256)} %constant.96) | copy-start | bytes 3076
  7.2 13.4 %copy-start.19 = (f32[8]{0:T(128)S(1)}, f32[8]{0:T(128)}, u32[]{:S(2)}) copy-start(f32[8]{0:T(128)} %param.16) | copy-start | bytes 100
  7.2 91.6 %all-gather.10.cloned.1.call-start = ((), (), s32[]{:S(2)}) async-start(), calls=%async_computation.3 | async-start | bytes 8650752 | tf_op jit(solution)/shard_map/all_gather | solution.py:15
  23.5 132.6 %all-gather.8.cloned.1.call-start = ((), (), s32[]{:S(2)}) async-start(), calls=%async_computation.1 | async-start | bytes 12976128 | tf_op jit(solution)/shard_map/all_gather | solution.py:167
  24.2 226.6 %all-gather.12.cloned.1.call-start = ((), (), s32[]{:S(2)}) async-start(), calls=%async_computation.4 | async-start | bytes 8650752 | tf_op jit(solution)/shard_map/all_gather | solution.py:15
  94.2 3.1 copy-start.9
  96.3 1.0 copy-start.13
  172.8 7.0 %copy-start.12 = (f32[256,8,128]{0,2,1:T(8,128)S(1)}, f32[256,8,128]{0,2,1:T(8,128)}, u32[]{:S(2)}) copy-start(f32[256,8,128]{0,2,1:T(8,128)} %get-tuple-element.186) | copy-start | bytes 3145732
  179.8 1.9 copy-start.6
  182.7 182.2 %reduce-scatter.4.cloned.1.call-start = ((), (), s32[]{:S(2)}) async-start(), calls=%async_computation.5 | async-start | bytes 12976128
  206.9 1.0 copy-start.5
  206.9 1.2 copy-start.10
  206.9 1.9 copy-start.18
  207.0 201.0 %all-reduce.5.cloned.1.call-start = ((), (), s32[]{:S(2)}) async-start(), calls=%async_computation.2 | async-start | bytes 1048576 | tf_op jit(solution)/shard_map/psum | solution.py:182
  208.1 1.2 copy-start.3
  208.8 1.0 copy-start.16
  208.8 2.0 copy-start.14
  209.3 2.8 copy-start.7
  210.8 1.3 copy-start.17
  250.9 116.1 %copy-start.11 = (bf16[32,8,8,128]{3,2,1,0:T(8,128)(2,1)S(1)}, bf16[32,8,8,128]{3,2,1,0:T(8,128)(2,1)}, u32[]{:S(2)}) copy-start(bf16[32,8,8,128]{3,2,1,0:T(8,128)(2,1)} %copy.85) | copy-start | bytes 1572868
  250.9 116.1 %copy-start.15 = (f32[256,8,128]{0,2,1:T(8,128)S(1)}, f32[256,8,128]{0,2,1:T(8,128)}, u32[]{:S(2)}) copy-start(f32[256,8,128]{0,2,1:T(8,128)} %convolution_bitcast_fusion.5) | copy-start | bytes 3145732
  285.9 81.1 %copy-start.2 = (f32[8,128,128]{2,1,0:T(8,128)}, f32[8,128,128]{2,1,0:T(8,128)S(1)}, u32[]{:S(2)}) copy-start(f32[8,128,128]{2,1,0:T(8,128)S(1)} %get-tuple-element.133) | copy-start | bytes 1572868
  368.1 44.3 %copy-start.1 = (bf16[1,256,6144]{2,1,0:T(8,128)(2,1)S(1)}, bf16[1,256,6144]{2,1,0:T(8,128)(2,1)}, u32[]{:S(2)}) copy-start(bf16[1,256,6144]{2,1,0:T(8,128)(2,1)} %param.14) | copy-start | bytes 9437188
  (2 other events, 1.6 us)
Sparse Core Ops, SparseCore 0:
  23.6 62.5 all-gather.9
  88.7 67.3 all-gather.7
  182.9 67.9 all-gather.11
  254.8 110.0 reduce-scatter.3
  367.6 40.3 all-reduce.4
where the time goes:
time: 422 us; the launch traced here: 419 us
  waiting for transfers between devices  201 us (48%)
  blocking collectives  66.1 us (16%)
  local copies, waits for them, and re-layouts  59 us (14%)
  other arithmetic  42.3 us (10%)
  matrix products  31.7 us (8%)
  between operations  17.3 us (4%)
    unnamed x6, waiting for transfers between devices  79.8 us
    unnamed x1, blocking collectives  66.1 us
    all_gather x1, waiting for transfers between devices, local(): lax.all_gather(out_weight, 'seq', axis=0, tiled=True)  51.4 us
    all_gather x2, waiting for transfers between devices, prefix(): lax.all_gather(a.astype(kind), axis)  37.4 us
    add x31, other arithmetic, combine_states(): later[0][:, None, None] * earlier[1] + later[1]  35.8 us
    unnamed x55, local copies, waits for them, and re-layouts  34.2 us
    psum x1, waiting for transfers between devices, local(): grad_weight = lax.psum(weight_part, 'dp').astype(jnp.float32) * norm_factor  32.9 us
    dot_general x1, local copies, waits for them, and re-layouts, local(): jnp.dot(columns, lax.all_gather(out_weight, 'seq', axis=0, tiled=True), p...  16.7 us
  transfers between devices with their start and end apart: 5, of which 4 were waited for; matrix products, arithmetic and copies ran while one was open for 20% of the time, Pallas kernels for 0%

commit v1 on v0

--- a/solution.py
+++ b/solution.py
@@ -179,7 +179,9 @@
         tiled=True,
     )
     norm_factor = (lax.axis_size("dp") * seq_count * tok_count) ** (-0.5)
-    grad_weight = lax.psum(weight_part, "dp").astype(jnp.float32) * norm_factor
+    grad_weight = (
+        jnp.sum(lax.all_gather(weight_part, "dp"), axis=0).astype(jnp.float32) * norm_factor
+    )
     grad_attn, grad_scores, back_local = backward_local(
         queries,
         values_here,

time: 422 us -> 389 us (0.922)
  waiting for transfers between devices: 201 us -> 160 us
  blocking collectives: 66.1 us -> 77.4 us
    unnamed x6 -> x4, waiting for transfers between devices: 79.8 us -> 0.74 us
    reduce_scatter x0 -> x1, waiting for transfers between devices: none -> 70 us  [local(): lax.psum_scatter(part.astype(jnp.bfloat16).astype(jnp.float32).astype(jnp...]
    psum x1 -> x0, waiting for transfers between devices: 32.9 us -> none  [local(): grad_weight = lax.psum(weight_part, 'dp').astype(jnp.float32) * norm_factor]
    all_gather x0 -> x1, blocking collectives: none -> 11.6 us  [local(): lax.all_gather(weight_part, 'dp')]
    unnamed x55 -> x53, local copies, waits for them, and re-layouts: 34.2 us -> 30.7 us
  transfers between devices with their start and end apart: 5 -> 4, of which waited for: 4 -> 3; matrix products, arithmetic and copies ran while one was open for 20% -> 22% of each run, Pallas kernels for 0% -> 0%
where the time goes in v1:
time: 389 us; the launch traced here: 386 us
  waiting for transfers between devices  160 us (41%)
  blocking collectives  77.4 us (20%)
  local copies, waits for them, and re-layouts  55.6 us (14%)
  other arithmetic  42.5 us (11%)
  matrix products  31.9 us (8%)
  between operations  17.3 us (4%)
    reduce_scatter x1, waiting for transfers between devices, local(): lax.psum_scatter(part.astype(jnp.bfloat16).astype(jnp.float32).astype(jnp...  70 us
    unnamed x1, blocking collectives  65.7 us
    all_gather x1, waiting for transfers between devices, local(): lax.all_gather(out_weight, 'seq', axis=0, tiled=True)  51.6 us
    all_gather x2, waiting for transfers between devices, prefix(): lax.all_gather(a.astype(kind), axis)  37.3 us
    add x31, other arithmetic, combine_states(): later[0][:, None, None] * earlier[1] + later[1]  35.8 us
    unnamed x53, local copies, waits for them, and re-layouts  30.7 us
    dot_general x1, local copies, waits for them, and re-layouts, local(): jnp.dot(columns, lax.all_gather(out_weight, 'seq', axis=0, tiled=True), p...  16.8 us
    all_gather x1, blocking collectives, local(): lax.all_gather(weight_part, 'dp')  11.6 us
  transfers between devices with their start and end apart: 4, of which 3 were waited for; matrix products, arithmetic and copies ran while one was open for 22% of the time, Pallas kernels for 0%

profile of v1, /device:TPU:1, one launch (start us, length us, event | category | flops | bytes accessed | tf_op | source)
XLA Modules:
  0.0 385.5 jit_solution(10837680581630956489)
XLA Ops:
  12.7 2.7 bitcast_compare_fusion.3
  15.4 1.9 copy.84
  17.3 2.1 copy.57
  21.4 2.0 convolution_convert_fusion.1
  26.0 65.7 %all-reduce.2 = (bf16[256]{0:T(256)(128)(2,1)S(1)}, bf16[256]{0:T(256)(128)(2,1)S(1)}) all-reduce(bf16[256]{0:T(256)(128)(2,1)S(1)} %dynamic-update-slice, bf16[256]{0:T(256)(128)(2,1)S(1)} %dynamic-update-slice.1), channel_id=2, replica_groups=mesh['dp'=2,'seq'=32,'head'=4] {'seq'}, use_global_device_ids=true, to_apply=%add | all-reduce | flops 512 | bytes 2048
  91.9 2.1 copy.83
  94.2 1.9 multiply_convert_fusion.1
  97.0 1.5 convolution_bitcast_fusion.7
  99.4 2.1 while.26
  99.4 2.1 convert_add_fusion.4
  101.5 3.0 multiply_reduce_fusion.1
  104.5 51.6 %all-gather.9.cloned.1.call-done = bf16[6144,1024]{1,0:T(8,128)(2,1)} async-done(((bf16[192,1024]{1,0:T(8,128)(2,1)}), bf16[6144,1024]{1,0:T(8,128)(2,1)}) %all-gather.9.cloned.1.call-update) | async-done | bytes 12582928 | tf_op jit(solution)/shard_map/all_gather | solution.py:167
  156.1 16.8 %copy.61 = bf16[1024,6144]{1,0:T(8,128)(2,1)} copy(bf16[1024,6144]{0,1:T(8,128)(2,1)} %bitcast.112) | data formatting | bytes 25165824 | tf_op jit(solution)/shard_map/dot_general | solution.py:165
  172.9 7.0 %multiply_reduce_fusion = (f32[256,8]{0,1:T(8,128)S(1)}, f32[256,8,128]{0,2,1:T(8,128)S(1)}) fusion(f32[256,8,128]{0,2,1:T(8,128)} %get-tuple-element.186, f32[256,8]{0,1:T(8,128)S(1)} %add_rsqrt_fusion, bf16[8,128,6144]{2,1,0:T(8,128)(2,1)} %bitcast.113, bf16[1,256,6144]{2,1,0:T(8,128)(2,1)S(1)} %copy-done), kind=kOutput, calls=%fused_computation.34 | convolution fusion | flops 3222009856 | bytes 17842176 | tf_op jit(solution)/shard_map/dot_general | solution.py:165
  182.9 7.5 %convert_bitcast_fusion = bf16[6144,1024]{0,1:T(8,128)(2,1)} fusion(bf16[256,1024]{0,1:T(8,128)(2,1)} %bitcast.129, bf16[1,256,6144]{2,1,0:T(8,128)(2,1)S(1)} %copy-done), kind=kOutput, calls=%fused_computation.4 | convolution fusion | flops 3227516928 | bytes 16252928 | tf_op jit(solution)/shard_map/dot_general | solution.py:172
  190.4 16.7 %copy.81 = bf16[6144,1024]{1,0:T(8,128)(2,1)} copy(bf16[6144,1024]{0,1:T(8,128)(2,1)} %convert_bitcast_fusion) | data formatting | bytes 25165824
  212.3 1.3 convolution_bitcast_fusion.4
  213.6 37.3 %all-gather.13.cloned.1.call-done = bf16[256,128,128]{2,1,0:T(8,128)(2,1)} async-done(((bf16[8,128,128]{2,1,0:T(8,128)(2,1)}), bf16[256,128,128]{2,1,0:T(8,128)(2,1)}) %all-gather.13.cloned.1.call-update) | async-done | bytes 8388624 | tf_op jit(solution)/shard_map/all_gather | solution.py:15
  251.0 35.0 %while.27 = (s32[]{:T(128)}, f32[8,128,128]{2,1,0:T(8,128)S(1)}, s32[]{:T(128)}, bf16[32,8]{1,0:T(8,128)(2,1)S(1)}, bf16[32,8,128,128]{3,2,1,0:T(8,128)(2,1)}, /*index=5*/s32[]{:T(128)}, s32[]{:T(128)}, s32[]{:T(128)}, s32[]{:T(128)}) while((s32[]{:T(128)}, f32[8,128,128]{2,1,0:T(8,128)S(1)}, s32[]{:T(128)}, bf16[32,8]{1,0:T(8,128)(2,1)S(1)}, ...), condition=%wide.region_5.6_spmd, body=%wide.region_4.5_spmd.sunk | while | flops 393230 | bytes 1310955 | solution.py:30
  288.0 2.2 copy.75
  290.2 2.8 fusion.12
  293.0 2.1 copy.74
  295.1 70.0 %reduce-scatter.4.cloned.1.call-done = bf16[192,1024]{1,0:T(8,128)(2,1)} async-done(((bf16[6144,1024]{1,0:T(8,128)(2,1)}), bf16[192,1024]{1,0:T(8,128)(2,1)}) %reduce-scatter.4.cloned.1.call-update) | async-done | bytes 393232 | tf_op jit(solution)/shard_map/reduce_scatter | solution.py:175
  365.1 11.6 %all-gather.4 = bf16[384,1024]{1,0:T(8,128)(2,1)} all-gather(bf16[192,1024]{1,0:T(8,128)(2,1)} %reduce-scatter.4.cloned.1.call-done), channel_id=6, replica_groups=mesh['dp'=2,'seq'=32,'head'=4] {'dp'}, dimensions={0}, use_global_device_ids=true | all-gather | bytes 1179648 | tf_op jit(solution)/shard_map/all_gather | solution.py:183
  (145 shorter events, 55.3 us)
Async XLA Ops:
  7.2 165.7 %copy-start = (bf16[1,256,6144]{2,1,0:T(8,128)(2,1)S(1)}, bf16[1,256,6144]{2,1,0:T(8,128)(2,1)}, u32[]{:S(2)}) copy-start(bf16[1,256,6144]{2,1,0:T(8,128)(2,1)} %param.14) | copy-start | bytes 9437188
  7.2 17.1 %copy-start.20 = (u32[256]{0:T(256)S(1)}, u32[256]{0:T(256)}, u32[]{:S(2)}) copy-start(u32[256]{0:T(256)} %constant.98) | copy-start | bytes 3076
  7.2 13.4 %copy-start.19 = (f32[8]{0:T(128)S(1)}, f32[8]{0:T(128)}, u32[]{:S(2)}) copy-start(f32[8]{0:T(128)} %param.16) | copy-start | bytes 100
  7.2 91.4 %all-gather.11.cloned.1.call-start = ((), (), s32[]{:S(2)}) async-start(), calls=%async_computation.2 | async-start | bytes 8650752 | tf_op jit(solution)/shard_map/all_gather | solution.py:15
  23.5 132.6 %all-gather.9.cloned.1.call-start = ((), (), s32[]{:S(2)}) async-start(), calls=%async_computation.1 | async-start | bytes 12976128 | tf_op jit(solution)/shard_map/all_gather | solution.py:167
  24.2 226.7 %all-gather.13.cloned.1.call-start = ((), (), s32[]{:S(2)}) async-start(), calls=%async_computation.3 | async-start | bytes 8650752 | tf_op jit(solution)/shard_map/all_gather | solution.py:15
  93.9 3.1 copy-start.9
  96.1 1.0 copy-start.13
  172.9 7.0 %copy-start.12 = (f32[256,8,128]{0,2,1:T(8,128)S(1)}, f32[256,8,128]{0,2,1:T(8,128)}, u32[]{:S(2)}) copy-start(f32[256,8,128]{0,2,1:T(8,128)} %get-tuple-element.186) | copy-start | bytes 3145732
  179.9 1.9 copy-start.6
  181.0 0.8 copy-start.4
  182.9 182.2 %reduce-scatter.4.cloned.1.call-start = ((), (), s32[]{:S(2)}) async-start(), calls=%async_computation.4 | async-start | bytes 12976128 | tf_op jit(solution)/shard_map/reduce_scatter | solution.py:175
  207.1 1.0 copy-start.5
  207.1 1.2 copy-start.10
  207.1 1.9 copy-start.18
  208.3 1.2 copy-start.3
  209.0 1.0 copy-start.16
  209.0 2.0 copy-start.14
  209.5 2.8 copy-start.7
  211.0 1.3 copy-start.17
  251.0 35.8 %copy-start.15 = (f32[256,8,128]{0,2,1:T(8,128)S(1)}, f32[256,8,128]{0,2,1:T(8,128)}, u32[]{:S(2)}) copy-start(f32[256,8,128]{0,2,1:T(8,128)} %convolution_bitcast_fusion.5) | copy-start | bytes 3145732
  251.0 35.8 %copy-start.11 = (bf16[32,8,8,128]{3,2,1,0:T(8,128)(2,1)S(1)}, bf16[32,8,8,128]{3,2,1,0:T(8,128)(2,1)}, u32[]{:S(2)}) copy-start(bf16[32,8,8,128]{3,2,1,0:T(8,128)(2,1)} %copy.84) | copy-start | bytes 1572868
  286.0 0.8 copy-start.2
  288.0 91.0 %copy-start.1 = (bf16[1,256,6144]{2,1,0:T(8,128)(2,1)S(1)}, bf16[1,256,6144]{2,1,0:T(8,128)(2,1)}, u32[]{:S(2)}) copy-start(bf16[1,256,6144]{2,1,0:T(8,128)(2,1)} %param.14) | copy-start | bytes 9437188
  (1 other events, 0.8 us)
Sparse Core Ops, SparseCore 0:
  23.6 62.4 all-gather.10
  88.7 67.3 all-gather.8
  183.0 67.9 all-gather.12
  255.0 110.0 reduce-scatter.3
